TPU v7x, 32 devices: a whole 2x2x4 slice. The times are simulated.
32 devices in a mesh: section: 2 (over x), gy: 4 (over y, core), gx: 4 (over z).
Axes of the slice: x: 2, y: 2, z: 4, core: 2. Of those that a mesh axis runs over, the one named last changes fastest.
Arguments:
- images: bfloat16 [2, 128, 256, 128], P('section', 'gy', 'gx'), may hold values from -6 to 6
- first_kernel: bfloat16 [3, 3, 128, 128], replicated, may hold values from -0.1875 to 0.1875
- projection: bfloat16 [128, 256], replicated, may hold values from -0.5 to 0.5
- second_kernel: bfloat16 [3, 3, 256, 256], replicated, may hold values from -0.125 to 0.125
- cotangent: bfloat16 [2, 64, 128, 256], P('section', 'gy', 'gx'), may hold values from -0.625 to 0.625
Outputs:
- features: bfloat16 [2, 64, 128, 256], P('section', 'gy', 'gx')
- grad_first: float32 [3, 3, 128, 128], replicated
- grad_projection: float32 [128, 256], replicated
- grad_second: float32 [3, 3, 256, 256], replicated
All inputs are finite; a program needn't handle non-finite values.
Results may differ from a plain program's by a relative error of at most 0.014.
Values may be sent and summed in bfloat16 or wider, within the bound.
No kernel may reach another device: no remote copies, remote signals or barrier semaphores. Data moves between devices by JAX's collectives and lax.ppermute only.
A program may use at most 64 MiB of HBM per device.

v0:
```python
import jax
import jax.numpy as jnp
from jax import lax
from jax.sharding import PartitionSpec as P


def padded_2(array, sides, width):
    for axis, dim in sides:
        size, length = (lax.axis_size(axis), array.shape[dim])
        up = [(i, (i + 1) % size) for i in range(size - 1)]
        down = [(j, i) for i, j in up]
        last = lax.slice_in_dim(array, length - width, length, axis=dim)
        initial = lax.slice_in_dim(array, 0, width, axis=dim)
        before = lax.ppermute(last, axis, up)
        after = lax.ppermute(initial, axis, down)
        array = jnp.concatenate([before, array, after], axis=dim)
    return array


def from_partner(block, axis, bit):
    count = lax.axis_size(axis)
    route = []
    for low in range(count):
        high = low | 1 << bit
        if high != low and high < count:
            route += [(low, high), (high, low)]
    return lax.ppermute(block, axis, route)


def silu_slope(values):
    sigma = jax.nn.sigmoid(values)
    return sigma * (1.0 + values * (1.0 - sigma))


def conv_forward(padded, kernel, row_count, col_count):
    total = jnp.zeros((row_count * col_count, kernel.shape[3]), jnp.float32)
    for row_tap in range(3):
        for col_tap in range(3):
            piece = padded[row_tap : row_tap + row_count, col_tap : col_tap + col_count].reshape(
                row_count * col_count, padded.shape[2]
            )
            total = total + jnp.dot(
                piece, kernel[row_tap, col_tap], preferred_element_type=jnp.float32
            )
    return total


def conv_slopes(padded, slope, row_count, col_count):
    pieces = []
    for row_tap in range(3):
        for col_tap in range(3):
            piece = padded[row_tap : row_tap + row_count, col_tap : col_tap + col_count].reshape(
                row_count * col_count, padded.shape[2]
            )
            pieces.append(jnp.einsum("pc,pd->cd", piece, slope, preferred_element_type=jnp.float32))
    return jnp.stack(pieces).reshape(3, 3, padded.shape[2], slope.shape[1])


def conv_back(padded, kernel, row_count, col_count):
    total = jnp.zeros((row_count * col_count, kernel.shape[2]), jnp.float32)
    for row_tap in range(3):
        for col_tap in range(3):
            piece = padded[
                2 - row_tap : 2 - row_tap + row_count, 2 - col_tap : 2 - col_tap + col_count
            ].reshape(row_count * col_count, padded.shape[2])
            total = total + jnp.einsum(
                "pd,cd->pc", piece, kernel[row_tap, col_tap], preferred_element_type=jnp.float32
            )
    return total


def first_forward(tile, first_kernel):
    row_count, col_count, channels = tile.shape
    padded = padded_2(tile, (("gy", 0), ("gx", 1)), 1)
    before = conv_forward(padded, first_kernel, row_count, col_count)
    hidden = jax.nn.silu(before).astype(jnp.bfloat16).reshape(row_count, col_count, channels)
    pooled = (
        hidden.astype(jnp.float32)
        .reshape(row_count // 2, 2, col_count // 2, 2, channels)
        .sum(axis=(1, 3))
        * 0.25
    ).astype(jnp.bfloat16)
    return (padded, before, pooled)


def project(pooled, projection):
    half_rows, half_cols, channels = pooled.shape
    flat = jnp.dot(
        pooled.reshape(half_rows * half_cols, channels),
        projection,
        preferred_element_type=jnp.float32,
    )
    return flat.astype(jnp.bfloat16).reshape(half_rows, half_cols, projection.shape[1])


def second_pass(middle, second_kernel, upstream):
    half_rows, half_cols, wide = middle.shape
    padded = padded_2(middle, (("gy", 0), ("gx", 1)), 1)
    before = conv_forward(padded, second_kernel, half_rows, half_cols)
    output = jax.nn.silu(before).astype(jnp.bfloat16).reshape(half_rows, half_cols, wide)
    flat_up = upstream.reshape(half_rows * half_cols, wide).astype(jnp.float32)
    slope = (flat_up * silu_slope(before)).astype(jnp.bfloat16)
    kernel_grad = conv_slopes(padded, slope, half_rows, half_cols)
    slope_padded = padded_2(slope.reshape(half_rows, half_cols, wide), (("gy", 0), ("gx", 1)), 1)
    back = conv_back(slope_padded, second_kernel, half_rows, half_cols).astype(jnp.bfloat16)
    return (output, kernel_grad, back.reshape(half_rows, half_cols, wide))


def projection_back(pooled, back, projection):
    half_rows, half_cols, channels = pooled.shape
    flat_pool = pooled.reshape(half_rows * half_cols, channels)
    flat_back = back.reshape(half_rows * half_cols, back.shape[2])
    grad = jnp.einsum("pc,pd->cd", flat_pool, flat_back, preferred_element_type=jnp.float32)
    pooled_slope = jnp.einsum(
        "pd,cd->pc", flat_back, projection, preferred_element_type=jnp.float32
    )
    return (grad, pooled_slope.astype(jnp.bfloat16).reshape(half_rows, half_cols, channels))


def first_back(padded, before, pooled_slope):
    half_rows, half_cols, channels = pooled_slope.shape
    spread = jnp.broadcast_to(
        (pooled_slope.astype(jnp.float32) * 0.25)[:, None, :, None, :],
        (half_rows, 2, half_cols, 2, channels),
    )
    spread = spread.reshape(4 * half_rows * half_cols, channels)
    slope = (spread * silu_slope(before)).astype(jnp.bfloat16)
    return conv_slopes(padded, slope, 2 * half_rows, 2 * half_cols)


def per_device(images, first_kernel, projection, second_kernel, cotangent):
    padded, before, pooled = first_forward(images[0], first_kernel)
    upstream = from_partner(cotangent[0], "section", 0)
    middle = project(pooled, projection)
    output, grad_second, back = second_pass(middle, second_kernel, upstream)
    grad_projection, pooled_slope = projection_back(pooled, back, projection)
    output = from_partner(output, "section", 0)
    grad_first = first_back(padded, before, pooled_slope)
    grad_first, grad_projection, grad_second = lax.psum(
        (grad_first, grad_projection, grad_second), ("section", "gy", "gx")
    )
    return (output[None], grad_first, grad_projection, grad_second)


def solution(mesh):
    placed = (P("section", "gy", "gx", None), P(), P(), P(), P("section", "gy", "gx", None))
    return jax.shard_map(
        per_device,
        mesh=mesh,
        in_specs=placed,
        out_specs=(P("section", "gy", "gx", None), P(), P(), P()),
        check_vma=False,
    )
```

profile of v0, /device:TPU:0, one launch (start us, length us, event | category | flops | bytes accessed | tf_op | source)
XLA Modules:
  0.0 227.4 jit_solution(3787896188777336523)
XLA Ops:
  8.0 2.4 %collective-permute-start = (bf16[1,64,128]{2,1,0:T(8,128)(2,1)S(1)}, bf16[1,64,128]{2,1,0:T(8,128)(2,1)S(1)}, u32[]{:S(2)}, u32[]{:S(2)}) collective-permute-start(bf16[1,64,128]{2,1,0:T(8,128)(2,1)S(1)} %get-tuple-element.21), channel_id=1, source_target_pairs={{0,4},{4,8},{8,12},{1,5},{5,9},{9,13},{2,6},{6,10},{10,14},{3,7},{... | collective-permute-start | bytes 49160 | tf_op jit(solution)/shard_map/ppermute | solution.py:14
  10.4 1.3 collective-permute-start.1
  11.7 3.9 %collective-permute-done.1 = bf16[1,64,128]{2,1,0:T(8,128)(2,1)S(1)} collective-permute-done((bf16[1,64,128]{2,1,0:T(8,128)(2,1)S(1)}, bf16[1,64,128]{2,1,0:T(8,128)(2,1)S(1)}, u32[]{:S(2)}, u32[]{:S(2)}) %collective-permute-start.1) | collective-permute-done | bytes 16416 | tf_op jit(solution)/shard_map/ppermute | solution.py:15
  16.5 3.5 %collective-permute-start.2 = (bf16[34,1,128]{2,1,0:T(2,128)(2,1)S(1)}, bf16[34,1,128]{2,1,0:T(2,128)(2,1)S(1)}, u32[]{:S(2)}, u32[]{:S(2)}) collective-permute-start(bf16[34,1,128]{2,1,0:T(2,128)(2,1)S(1)} %get-tuple-element.15), channel_id=1, source_target_pairs={{0,1},{1,2},{2,3},{4,5},{5,6},{6,7},{8,9},{9,10},{10,11},{12,13},{... | collective-permute-start | bytes 26120 | tf_op jit(solution)/shard_map/ppermute | solution.py:14
  20.0 1.4 collective-permute-start.3
  21.5 1.3 pad_maximum_fusion.1
  23.1 2.8 %collective-permute-done.3 = bf16[34,1,128]{2,1,0:T(2,128)(2,1)S(1)} collective-permute-done((bf16[34,1,128]{2,1,0:T(2,128)(2,1)S(1)}, bf16[34,1,128]{2,1,0:T(2,128)(2,1)S(1)}, u32[]{:S(2)}, u32[]{:S(2)}) %collective-permute-start.3) | collective-permute-done | bytes 8736 | tf_op jit(solution)/shard_map/ppermute | solution.py:15
  30.4 3.0 %collective-permute-start.4 = (bf16[1,32,256]{2,1,0:T(8,128)(2,1)S(1)}, bf16[1,32,256]{2,1,0:T(8,128)(2,1)S(1)}, u32[]{:S(2)}, u32[]{:S(2)}) collective-permute-start(bf16[1,32,256]{2,1,0:T(8,128)(2,1)S(1)} %get-tuple-element.49), channel_id=1, source_target_pairs={{0,4},{4,8},{8,12},{1,5},{5,9},{9,13},{2,6},{6,10},{10,14},{3,7},{... | collective-permute-start | bytes 49160 | tf_op jit(solution)/shard_map/ppermute | solution.py:14
  33.4 1.3 collective-permute-start.5
  34.7 1.6 collective-permute-start.9
  36.3 1.2 collective-permute-done.5
  37.5 3.5 %collective-permute-start.6 = (bf16[18,1,256]{2,1,0:T(2,128)(2,1)S(1)}, bf16[18,1,256]{2,1,0:T(2,128)(2,1)S(1)}, u32[]{:S(2)}, u32[]{:S(2)}) collective-permute-start(bf16[18,1,256]{2,1,0:T(2,128)(2,1)S(1)} %get-tuple-element.41), channel_id=1, source_target_pairs={{0,1},{1,2},{2,3},{4,5},{5,6},{6,7},{8,9},{9,10},{10,11},{12,13},{... | collective-permute-start | bytes 27656 | tf_op jit(solution)/shard_map/ppermute | solution.py:14
  40.9 1.3 collective-permute-start.7
  42.5 4.1 %collective-permute-done.7 = bf16[18,1,256]{2,1,0:T(2,128)(2,1)S(1)} collective-permute-done((bf16[18,1,256]{2,1,0:T(2,128)(2,1)S(1)}, bf16[18,1,256]{2,1,0:T(2,128)(2,1)S(1)}, u32[]{:S(2)}, u32[]{:S(2)}) %collective-permute-start.7) | collective-permute-done | bytes 9248 | tf_op jit(solution)/shard_map/ppermute | solution.py:15
  49.4 3.2 %collective-permute-start.10 = (bf16[1,32,256]{2,1,0:T(8,128)(2,1)S(1)}, bf16[1,32,256]{2,1,0:T(8,128)(2,1)S(1)}, u32[]{:S(2)}, u32[]{:S(2)}) collective-permute-start(bf16[1,32,256]{2,1,0:T(8,128)(2,1)S(1)} %get-tuple-element.45), channel_id=1, source_target_pairs={{0,4},{4,8},{8,12},{1,5},{5,9},{9,13},{2,6},{6,10},{10,14},{3,7},{... | collective-permute-start | bytes 49160 | tf_op jit(solution)/shard_map/ppermute | solution.py:14
  52.6 1.3 collective-permute-start.11
  56.5 1.3 collective-permute-start.12
  57.8 4.7 %collective-permute-start.13 = (bf16[18,1,256]{2,1,0:T(2,128)(2,1)S(1)}, bf16[18,1,256]{2,1,0:T(2,128)(2,1)S(1)}, u32[]{:S(2)}, u32[]{:S(2)}) collective-permute-start(bf16[18,1,256]{2,1,0:T(2,128)(2,1)S(1)} %get-tuple-element.38), channel_id=1, source_target_pairs={{0,1},{1,2},{2,3},{4,5},{5,6},{6,7},{8,9},{9,10},{10,11},{12,13},{... | collective-permute-start | bytes 27656 | tf_op jit(solution)/shard_map/ppermute | solution.py:14
  62.9 0.9 collective-permute-done.13
  72.5 1.4 collective-permute-start.8
  73.9 7.5 %collective-permute-done.8 = bf16[16,32,256]{2,1,0:T(8,128)(2,1)S(1)} collective-permute-done((bf16[16,32,256]{2,1,0:T(8,128)(2,1)S(1)}, bf16[16,32,256]{2,1,0:T(8,128)(2,1)S(1)}, u32[]{:S(2)}, u32[]{:S(2)}) %collective-permute-start.8) | collective-permute-done | bytes 262176 | tf_op jit(solution)/shard_map/ppermute | solution.py:27
  81.3 132.7 %all-reduce.3.cloned.1.call-done = (f32[3,3,128,128]{3,2,1,0:T(8,128)}, f32[128,256]{1,0:T(8,128)}, f32[3,3,256,256]{3,2,1,0:T(8,128)}) async-done(((f32[3,3,128,128]{3,2,1,0:T(8,128)}, f32[128,256]{1,0:T(8,128)}, f32[3,3,256,256]{3,2,1,0:T(8,128)}), (f32[3,3,128,128]{3,2,1,0:T(8,128)}, f32[128,256]{1,0:T(8,128)}, f32[3,3,256,256]{3,2,1,0:T(8,128)})) %all-reduce.3.cloned.1.call-update) | async-done | bytes 3080208 | tf_op jit(solution)/shard_map/psum | solution.py:139
  214.8 1.9 copy.32
  217.3 3.2 %copy.34 = f32[3,3,256,256]{3,2,1,0:T(8,128)} copy(f32[3,3,256,256]{3,2,1,0:T(8,128)} %get-tuple-element.63) | data formatting | bytes 4718592
  (96 shorter events, 22.2 us)
Async XLA Ops:
  7.2 23.0 %copy-start = (bf16[128,256]{1,0:T(8,128)(2,1)S(1)}, bf16[128,256]{1,0:T(8,128)(2,1)}, u32[]{:S(2)}) copy-start(bf16[128,256]{1,0:T(8,128)(2,1)} %param.7) | copy-start | bytes 196612
  7.2 15.6 %copy-start.5 = (bf16[3,3,128,128]{3,2,1,0:T(8,128)(2,1)S(1)}, bf16[3,3,128,128]{3,2,1,0:T(8,128)(2,1)}, u32[]{:S(2)}) copy-start(bf16[3,3,128,128]{3,2,1,0:T(8,128)(2,1)} %param.6) | copy-start | bytes 884740
  7.2 206.9 %all-reduce.3.cloned.1.call-start = ((), (), s32[]{:S(2)}) async-start(), calls=%async_computation | async-start | bytes 6160384 | tf_op jit(solution)/shard_map/psum | solution.py:139
  8.0 3.7 %collective-permute-start = (bf16[1,64,128]{2,1,0:T(8,128)(2,1)S(1)}, bf16[1,64,128]{2,1,0:T(8,128)(2,1)S(1)}, u32[]{:S(2)}, u32[]{:S(2)}) collective-permute-start(bf16[1,64,128]{2,1,0:T(8,128)(2,1)S(1)} %get-tuple-element.21), channel_id=1, source_target_pairs={{0,4},{4,8},{8,12},{1,5},{5,9},{9,13},{2,6},{6,10},{10,14},{3,7},{... | collective-permute-start | bytes 49160 | tf_op jit(solution)/shard_map/ppermute | solution.py:14
  10.4 5.2 %collective-permute-start.1 = (bf16[1,64,128]{2,1,0:T(8,128)(2,1)S(1)}, bf16[1,64,128]{2,1,0:T(8,128)(2,1)S(1)}, u32[]{:S(2)}, u32[]{:S(2)}) collective-permute-start(bf16[1,64,128]{2,1,0:T(8,128)(2,1)S(1)} %get-tuple-element.22), channel_id=1, source_target_pairs={{4,0},{8,4},{12,8},{5,1},{9,5},{13,9},{6,2},{10,6},{14,10},{7,3},{... | collective-permute-start | bytes 49160 | tf_op jit(solution)/shard_map/ppermute | solution.py:15
  16.5 6.5 %collective-permute-start.2 = (bf16[34,1,128]{2,1,0:T(2,128)(2,1)S(1)}, bf16[34,1,128]{2,1,0:T(2,128)(2,1)S(1)}, u32[]{:S(2)}, u32[]{:S(2)}) collective-permute-start(bf16[34,1,128]{2,1,0:T(2,128)(2,1)S(1)} %get-tuple-element.15), channel_id=1, source_target_pairs={{0,1},{1,2},{2,3},{4,5},{5,6},{6,7},{8,9},{9,10},{10,11},{12,13},{... | collective-permute-start | bytes 26120 | tf_op jit(solution)/shard_map/ppermute | solution.py:14
  20.0 5.8 %copy-start.1 = (bf16[1,32,64,128]{3,2,1,0:T(8,128)(2,1)S(1)}, bf16[1,32,64,128]{3,2,1,0:T(8,128)(2,1)}, u32[]{:S(2)}) copy-start(bf16[1,32,64,128]{3,2,1,0:T(8,128)(2,1)} %param.5) | copy-start | bytes 1572868
  20.0 5.8 %collective-permute-start.3 = (bf16[34,1,128]{2,1,0:T(2,128)(2,1)S(1)}, bf16[34,1,128]{2,1,0:T(2,128)(2,1)S(1)}, u32[]{:S(2)}, u32[]{:S(2)}) collective-permute-start(bf16[34,1,128]{2,1,0:T(2,128)(2,1)S(1)} %get-tuple-element.16), channel_id=1, source_target_pairs={{1,0},{2,1},{3,2},{5,4},{6,5},{7,6},{9,8},{10,9},{11,10},{13,12},{... | collective-permute-start | bytes 26120 | tf_op jit(solution)/shard_map/ppermute | solution.py:15
  29.2 5.4 %copy-start.7 = (bf16[1,16,32,256]{3,2,1,0:T(8,128)(2,1)S(1)}, bf16[1,16,32,256]{3,2,1,0:T(8,128)(2,1)}, u32[]{:S(2)}) copy-start(bf16[1,16,32,256]{3,2,1,0:T(8,128)(2,1)} %param.9) | copy-start | bytes 786436
  29.3 13.0 %copy-start.2 = (bf16[3,3,256,256]{3,2,1,0:T(8,128)(2,1)S(1)}, bf16[3,3,256,256]{3,2,1,0:T(8,128)(2,1)}, u32[]{:S(2)}) copy-start(bf16[3,3,256,256]{3,2,1,0:T(8,128)(2,1)} %param.8) | copy-start | bytes 3538948
  30.4 5.9 %collective-permute-start.4 = (bf16[1,32,256]{2,1,0:T(8,128)(2,1)S(1)}, bf16[1,32,256]{2,1,0:T(8,128)(2,1)S(1)}, u32[]{:S(2)}, u32[]{:S(2)}) collective-permute-start(bf16[1,32,256]{2,1,0:T(8,128)(2,1)S(1)} %get-tuple-element.49), channel_id=1, source_target_pairs={{0,4},{4,8},{8,12},{1,5},{5,9},{9,13},{2,6},{6,10},{10,14},{3,7},{... | collective-permute-start | bytes 49160 | tf_op jit(solution)/shard_map/ppermute | solution.py:14
  33.4 4.0 %collective-permute-start.5 = (bf16[1,32,256]{2,1,0:T(8,128)(2,1)S(1)}, bf16[1,32,256]{2,1,0:T(8,128)(2,1)S(1)}, u32[]{:S(2)}, u32[]{:S(2)}) collective-permute-start(bf16[1,32,256]{2,1,0:T(8,128)(2,1)S(1)} %get-tuple-element.50), channel_id=1, source_target_pairs={{4,0},{8,4},{12,8},{5,1},{9,5},{13,9},{6,2},{10,6},{14,10},{7,3},{... | collective-permute-start | bytes 49160 | tf_op jit(solution)/shard_map/ppermute | solution.py:15
  34.7 14.0 %collective-permute-start.9 = (bf16[16,32,256]{2,1,0:T(8,128)(2,1)S(1)}, bf16[16,32,256]{2,1,0:T(8,128)(2,1)S(1)}, u32[]{:S(2)}, u32[]{:S(2)}) collective-permute-start(bf16[16,32,256]{2,1,0:T(8,128)(2,1)S(1)} %bitcast.331), channel_id=1, source_target_pairs={{0,16},{16,0},{1,17},{17,1},{2,18},{18,2},{3,19},{19,3},{4,20},{20... | collective-permute-start | bytes 786440 | tf_op jit(solution)/shard_map/ppermute | solution.py:27
  37.5 5.1 %collective-permute-start.6 = (bf16[18,1,256]{2,1,0:T(2,128)(2,1)S(1)}, bf16[18,1,256]{2,1,0:T(2,128)(2,1)S(1)}, u32[]{:S(2)}, u32[]{:S(2)}) collective-permute-start(bf16[18,1,256]{2,1,0:T(2,128)(2,1)S(1)} %get-tuple-element.41), channel_id=1, source_target_pairs={{0,1},{1,2},{2,3},{4,5},{5,6},{6,7},{8,9},{9,10},{10,11},{12,13},{... | collective-permute-start | bytes 27656 | tf_op jit(solution)/shard_map/ppermute | solution.py:14
  40.9 5.7 %collective-permute-start.7 = (bf16[18,1,256]{2,1,0:T(2,128)(2,1)S(1)}, bf16[18,1,256]{2,1,0:T(2,128)(2,1)S(1)}, u32[]{:S(2)}, u32[]{:S(2)}) collective-permute-start(bf16[18,1,256]{2,1,0:T(2,128)(2,1)S(1)} %get-tuple-element.42), channel_id=1, source_target_pairs={{1,0},{2,1},{3,2},{5,4},{6,5},{7,6},{9,8},{10,9},{11,10},{13,12},{... | collective-permute-start | bytes 27656 | tf_op jit(solution)/shard_map/ppermute | solution.py:15
  49.4 6.8 %collective-permute-start.10 = (bf16[1,32,256]{2,1,0:T(8,128)(2,1)S(1)}, bf16[1,32,256]{2,1,0:T(8,128)(2,1)S(1)}, u32[]{:S(2)}, u32[]{:S(2)}) collective-permute-start(bf16[1,32,256]{2,1,0:T(8,128)(2,1)S(1)} %get-tuple-element.45), channel_id=1, source_target_pairs={{0,4},{4,8},{8,12},{1,5},{5,9},{9,13},{2,6},{6,10},{10,14},{3,7},{... | collective-permute-start | bytes 49160 | tf_op jit(solution)/shard_map/ppermute | solution.py:14
  52.6 3.9 %collective-permute-start.11 = (bf16[1,32,256]{2,1,0:T(8,128)(2,1)S(1)}, bf16[1,32,256]{2,1,0:T(8,128)(2,1)S(1)}, u32[]{:S(2)}, u32[]{:S(2)}) collective-permute-start(bf16[1,32,256]{2,1,0:T(8,128)(2,1)S(1)} %get-tuple-element.46), channel_id=1, source_target_pairs={{4,0},{8,4},{12,8},{5,1},{9,5},{13,9},{6,2},{10,6},{14,10},{7,3},{... | collective-permute-start | bytes 49160 | tf_op jit(solution)/shard_map/ppermute | solution.py:15
  56.1 7.9 %copy-start.3 = (f32[9,256,256]{2,1,0:T(8,128)}, f32[9,256,256]{2,1,0:T(8,128)S(1)}, u32[]{:S(2)}) copy-start(f32[9,256,256]{2,1,0:T(8,128)S(1)} %fusion.4) | copy-start | bytes 7077892
  56.5 6.3 %collective-permute-start.12 = (bf16[18,1,256]{2,1,0:T(2,128)(2,1)S(1)}, bf16[18,1,256]{2,1,0:T(2,128)(2,1)S(1)}, u32[]{:S(2)}, u32[]{:S(2)}) collective-permute-start(bf16[18,1,256]{2,1,0:T(2,128)(2,1)S(1)} %get-tuple-element.37), channel_id=1, source_target_pairs={{1,0},{2,1},{3,2},{5,4},{6,5},{7,6},{9,8},{10,9},{11,10},{13,12},{... | collective-permute-start | bytes 27656 | tf_op jit(solution)/shard_map/ppermute | solution.py:15
  57.8 6.0 %collective-permute-start.13 = (bf16[18,1,256]{2,1,0:T(2,128)(2,1)S(1)}, bf16[18,1,256]{2,1,0:T(2,128)(2,1)S(1)}, u32[]{:S(2)}, u32[]{:S(2)}) collective-permute-start(bf16[18,1,256]{2,1,0:T(2,128)(2,1)S(1)} %get-tuple-element.38), channel_id=1, source_target_pairs={{0,1},{1,2},{2,3},{4,5},{5,6},{6,7},{8,9},{9,10},{10,11},{12,13},{... | collective-permute-start | bytes 27656 | tf_op jit(solution)/shard_map/ppermute | solution.py:14
  71.6 0.8 copy-start.4
  72.5 8.9 %collective-permute-start.8 = (bf16[16,32,256]{2,1,0:T(8,128)(2,1)S(1)}, bf16[16,32,256]{2,1,0:T(8,128)(2,1)S(1)}, u32[]{:S(2)}, u32[]{:S(2)}) collective-permute-start(bf16[16,32,256]{2,1,0:T(8,128)(2,1)S(1)} %bitcast.332), channel_id=1, source_target_pairs={{0,16},{16,0},{1,17},{17,1},{2,18},{18,2},{3,19},{19,3},{4,20},{20... | collective-permute-start | bytes 786440 | tf_op jit(solution)/shard_map/ppermute | solution.py:27
  214.0 2.6 %copy-start.6 = (f32[128,256]{1,0:T(8,128)S(1)}, f32[128,256]{1,0:T(8,128)}, u32[]{:S(2)}) copy-start(f32[128,256]{1,0:T(8,128)} %get-tuple-element.62) | copy-start | bytes 393220
Sparse Core Ops, SparseCore 0:
  72.6 141.4 all-reduce.2
where the time goes:
time: 228 us; the launch traced here: 227 us
  waiting for transfers between devices  153 us (67%)
  starting transfers between devices  31.2 us (14%)
  between operations  14.7 us (6%)
  matrix products  14.2 us (6%)
  local copies, waits for them, and re-layouts  9.64 us (4%)
  other arithmetic  4.38 us (2%)
    psum x1, waiting for transfers between devices, per_device(): lax.psum((grad_first, grad_projection, grad_second), ('section', 'gy', 'g...  133 us
    ppermute x6, starting transfers between devices, padded_2(): before = lax.ppermute(last, axis, up)  20.3 us
    ppermute x6, waiting for transfers between devices, padded_2(): after = lax.ppermute(initial, axis, down)  12.2 us
    ppermute x6, starting transfers between devices, padded_2(): after = lax.ppermute(initial, axis, down)  7.88 us
    ppermute x2, waiting for transfers between devices, from_partner(): return lax.ppermute(block, axis, route)  7.47 us
    unnamed x20, local copies, waits for them, and re-layouts  7.35 us
    dot_general x18, matrix products, conv_slopes(): jnp.einsum('pc,pd->cd', piece, slope, preferred_element_type=jnp.float32)  5.6 us
    dot_general x18, matrix products, conv_forward(): jnp.dot(piece, kernel[row_tap, col_tap], preferred_element_type=jnp.float32)  4.91 us
  transfers between devices with their start and end apart: 15, of which 8 were waited for; matrix products, arithmetic and copies ran while one was open for 3% of the time, Pallas kernels for 0%

commit v1 on v0

--- a/solution.py
+++ b/solution.py
@@ -137,7 +137,7 @@
     output = from_partner(output, "section", 0)
     grad_first = first_back(padded, before, pooled_slope)
     grad_first, grad_projection, grad_second = lax.psum(
-        (grad_first, grad_projection, grad_second), ("section", "gy", "gx")
+        lax.psum((grad_first, grad_projection, grad_second), ("gy", "gx")), "section"
     )
     return (output[None], grad_first, grad_projection, grad_second)
 

time: 228 us -> 280 us (1.23)
  waiting for transfers between devices: 153 us -> 205 us
    psum x1 -> x2, waiting for transfers between devices: 133 us -> 187 us  [the longest x1 107 us: per_device(): lax.psum((grad_first, grad_projection, grad_second), ('gy', 'gx'))]
  transfers between devices with their start and end apart: 15 -> 16, of which waited for: 8 -> 9; matrix products, arithmetic and copies ran while one was open for 3% -> 2% of each run, Pallas kernels for 0% -> 0%
where the time goes in v1:
time: 280 us; the launch traced here: 279 us
  waiting for transfers between devices  205 us (73%)
  starting transfers between devices  31.3 us (11%)
  between operations  14.7 us (5%)
  matrix products  14.2 us (5%)
  local copies, waits for them, and re-layouts  9.64 us (3%)
  other arithmetic  4.4 us (2%)
    psum x1, waiting for transfers between devices, per_device(): lax.psum((grad_first, grad_projection, grad_second), ('gy', 'gx'))  107 us
    psum x1, waiting for transfers between devices, per_device(): lax.psum(lax.psum((grad_first, grad_projection, grad_second), ('gy', 'gx'...  79.5 us
    ppermute x6, starting transfers between devices, padded_2(): before = lax.ppermute(last, axis, up)  20.3 us
    ppermute x6, waiting for transfers between devices, padded_2(): after = lax.ppermute(initial, axis, down)  12.2 us
    ppermute x6, starting transfers between devices, padded_2(): after = lax.ppermute(initial, axis, down)  7.88 us
    unnamed x20, local copies, waits for them, and re-layouts  7.35 us
  transfers between devices with their start and end apart: 16, of which 9 were waited for; matrix products, arithmetic and copies ran while one was open for 2% of the time, Pallas kernels for 0%

profile of v1, /device:TPU:0, one launch (start us, length us, event | category | flops | bytes accessed | tf_op | source)
XLA Modules:
  0.0 279.1 jit_solution(2377744694106294687)
XLA Ops:
  8.0 2.4 collective-permute-start
  10.4 1.3 collective-permute-start.1
  11.7 3.9 %collective-permute-done.1 = bf16[1,64,128]{2,1,0:T(8,128)(2,1)S(1)} collective-permute-done((bf16[1,64,128]{2,1,0:T(8,128)(2,1)S(1)}, bf16[1,64,128]{2,1,0:T(8,128)(2,1)S(1)}, u32[]{:S(2)}, u32[]{:S(2)}) %collective-permute-start.1) | collective-permute-done | bytes 16416 | tf_op jit(solution)/shard_map/ppermute | solution.py:15
  16.5 3.5 %collective-permute-start.2 = (bf16[34,1,128]{2,1,0:T(2,128)(2,1)S(1)}, bf16[34,1,128]{2,1,0:T(2,128)(2,1)S(1)}, u32[]{:S(2)}, u32[]{:S(2)}) collective-permute-start(bf16[34,1,128]{2,1,0:T(2,128)(2,1)S(1)} %get-tuple-element.18), channel_id=1, source_target_pairs={{0,1},{1,2},{2,3},{4,5},{5,6},{6,7},{8,9},{9,10},{10,11},{12,13},{... | collective-permute-start | bytes 26120 | tf_op jit(solution)/shard_map/ppermute | solution.py:14
  20.0 1.4 collective-permute-start.3
  21.5 1.3 pad_maximum_fusion.1
  23.1 2.7 collective-permute-done.3
  30.4 3.0 %collective-permute-start.4 = (bf16[1,32,256]{2,1,0:T(8,128)(2,1)S(1)}, bf16[1,32,256]{2,1,0:T(8,128)(2,1)S(1)}, u32[]{:S(2)}, u32[]{:S(2)}) collective-permute-start(bf16[1,32,256]{2,1,0:T(8,128)(2,1)S(1)} %get-tuple-element.52), channel_id=1, source_target_pairs={{0,4},{4,8},{8,12},{1,5},{5,9},{9,13},{2,6},{6,10},{10,14},{3,7},{... | collective-permute-start | bytes 49160 | tf_op jit(solution)/shard_map/ppermute | solution.py:14
  33.4 1.3 collective-permute-start.5
  34.7 1.6 collective-permute-start.9
  36.3 1.2 collective-permute-done.5
  37.5 3.5 %collective-permute-start.6 = (bf16[18,1,256]{2,1,0:T(2,128)(2,1)S(1)}, bf16[18,1,256]{2,1,0:T(2,128)(2,1)S(1)}, u32[]{:S(2)}, u32[]{:S(2)}) collective-permute-start(bf16[18,1,256]{2,1,0:T(2,128)(2,1)S(1)} %get-tuple-element.44), channel_id=1, source_target_pairs={{0,1},{1,2},{2,3},{4,5},{5,6},{6,7},{8,9},{9,10},{10,11},{12,13},{... | collective-permute-start | bytes 27656 | tf_op jit(solution)/shard_map/ppermute | solution.py:14
  40.9 1.3 collective-permute-start.7
  42.5 4.1 %collective-permute-done.7 = bf16[18,1,256]{2,1,0:T(2,128)(2,1)S(1)} collective-permute-done((bf16[18,1,256]{2,1,0:T(2,128)(2,1)S(1)}, bf16[18,1,256]{2,1,0:T(2,128)(2,1)S(1)}, u32[]{:S(2)}, u32[]{:S(2)}) %collective-permute-start.7) | collective-permute-done | bytes 9248 | tf_op jit(solution)/shard_map/ppermute | solution.py:15
  49.4 3.2 %collective-permute-start.10 = (bf16[1,32,256]{2,1,0:T(8,128)(2,1)S(1)}, bf16[1,32,256]{2,1,0:T(8,128)(2,1)S(1)}, u32[]{:S(2)}, u32[]{:S(2)}) collective-permute-start(bf16[1,32,256]{2,1,0:T(8,128)(2,1)S(1)} %get-tuple-element.48), channel_id=1, source_target_pairs={{0,4},{4,8},{8,12},{1,5},{5,9},{9,13},{2,6},{6,10},{10,14},{3,7},{... | collective-permute-start | bytes 49160 | tf_op jit(solution)/shard_map/ppermute | solution.py:14
  52.6 1.3 collective-permute-start.11
  56.5 1.3 collective-permute-start.12
  57.8 4.7 %collective-permute-start.13 = (bf16[18,1,256]{2,1,0:T(2,128)(2,1)S(1)}, bf16[18,1,256]{2,1,0:T(2,128)(2,1)S(1)}, u32[]{:S(2)}, u32[]{:S(2)}) collective-permute-start(bf16[18,1,256]{2,1,0:T(2,128)(2,1)S(1)} %get-tuple-element.41), channel_id=1, source_target_pairs={{0,1},{1,2},{2,3},{4,5},{5,6},{6,7},{8,9},{9,10},{10,11},{12,13},{... | collective-permute-start | bytes 27656 | tf_op jit(solution)/shard_map/ppermute | solution.py:14
  72.5 107.0 %all-reduce.5.cloned.1.call-done = (f32[3,3,128,128]{3,2,1,0:T(8,128)}, f32[128,256]{1,0:T(8,128)}, f32[3,3,256,256]{3,2,1,0:T(8,128)}) async-done(((f32[3,3,128,128]{3,2,1,0:T(8,128)}, f32[128,256]{1,0:T(8,128)}, f32[3,3,256,256]{3,2,1,0:T(8,128)}), (f32[3,3,128,128]{3,2,1,0:T(8,128)}, f32[128,256]{1,0:T(8,128)}, f32[3,3,256,256]{3,2,1,0:T(8,128)})) %all-reduce.5.cloned.1.call-update) | async-done | bytes 3080208 | tf_op jit(solution)/shard_map/psum | solution.py:140
  179.5 1.5 collective-permute-start.8
  181.1 5.2 %collective-permute-done.8 = bf16[16,32,256]{2,1,0:T(8,128)(2,1)S(1)} collective-permute-done((bf16[16,32,256]{2,1,0:T(8,128)(2,1)S(1)}, bf16[16,32,256]{2,1,0:T(8,128)(2,1)S(1)}, u32[]{:S(2)}, u32[]{:S(2)}) %collective-permute-start.8) | collective-permute-done | bytes 262176 | tf_op jit(solution)/shard_map/ppermute | solution.py:27
  186.3 79.5 %all-reduce.7.cloned.1.call-done = (f32[3,3,128,128]{3,2,1,0:T(8,128)}, f32[128,256]{1,0:T(8,128)}, f32[3,3,256,256]{3,2,1,0:T(8,128)}) async-done(((f32[3,3,128,128]{3,2,1,0:T(8,128)}, f32[128,256]{1,0:T(8,128)}, f32[3,3,256,256]{3,2,1,0:T(8,128)}), (f32[3,3,128,128]{3,2,1,0:T(8,128)}, f32[128,256]{1,0:T(8,128)}, f32[3,3,256,256]{3,2,1,0:T(8,128)})) %all-reduce.7.cloned.1.call-update) | async-done | bytes 3080208 | tf_op jit(solution)/shard_map/psum | solution.py:139
  266.5 1.9 copy.35
  269.0 3.2 %copy.37 = f32[3,3,256,256]{3,2,1,0:T(8,128)} copy(f32[3,3,256,256]{3,2,1,0:T(8,128)} %get-tuple-element.66) | data formatting | bytes 4718592
  (99 shorter events, 23.2 us)
Async XLA Ops:
  7.2 23.0 %copy-start = (bf16[128,256]{1,0:T(8,128)(2,1)S(1)}, bf16[128,256]{1,0:T(8,128)(2,1)}, u32[]{:S(2)}) copy-start(bf16[128,256]{1,0:T(8,128)(2,1)} %param.7) | copy-start | bytes 196612
  7.2 15.6 %copy-start.5 = (bf16[3,3,128,128]{3,2,1,0:T(8,128)(2,1)S(1)}, bf16[3,3,128,128]{3,2,1,0:T(8,128)(2,1)}, u32[]{:S(2)}) copy-start(bf16[3,3,128,128]{3,2,1,0:T(8,128)(2,1)} %param.6) | copy-start | bytes 884740
  7.2 172.3 %all-reduce.5.cloned.1.call-start = ((), (), s32[]{:S(2)}) async-start(), calls=%async_computation | async-start | bytes 6160384 | tf_op jit(solution)/shard_map/psum | solution.py:140
  8.0 3.7 %collective-permute-start = (bf16[1,64,128]{2,1,0:T(8,128)(2,1)S(1)}, bf16[1,64,128]{2,1,0:T(8,128)(2,1)S(1)}, u32[]{:S(2)}, u32[]{:S(2)}) collective-permute-start(bf16[1,64,128]{2,1,0:T(8,128)(2,1)S(1)} %get-tuple-element.24), channel_id=1, source_target_pairs={{0,4},{4,8},{8,12},{1,5},{5,9},{9,13},{2,6},{6,10},{10,14},{3,7},{... | collective-permute-start | bytes 49160 | tf_op jit(solution)/shard_map/ppermute | solution.py:14
  10.4 5.2 %collective-permute-start.1 = (bf16[1,64,128]{2,1,0:T(8,128)(2,1)S(1)}, bf16[1,64,128]{2,1,0:T(8,128)(2,1)S(1)}, u32[]{:S(2)}, u32[]{:S(2)}) collective-permute-start(bf16[1,64,128]{2,1,0:T(8,128)(2,1)S(1)} %get-tuple-element.25), channel_id=1, source_target_pairs={{4,0},{8,4},{12,8},{5,1},{9,5},{13,9},{6,2},{10,6},{14,10},{7,3},{... | collective-permute-start | bytes 49160 | tf_op jit(solution)/shard_map/ppermute | solution.py:15
  16.5 6.5 %collective-permute-start.2 = (bf16[34,1,128]{2,1,0:T(2,128)(2,1)S(1)}, bf16[34,1,128]{2,1,0:T(2,128)(2,1)S(1)}, u32[]{:S(2)}, u32[]{:S(2)}) collective-permute-start(bf16[34,1,128]{2,1,0:T(2,128)(2,1)S(1)} %get-tuple-element.18), channel_id=1, source_target_pairs={{0,1},{1,2},{2,3},{4,5},{5,6},{6,7},{8,9},{9,10},{10,11},{12,13},{... | collective-permute-start | bytes 26120 | tf_op jit(solution)/shard_map/ppermute | solution.py:14
  20.0 5.8 %copy-start.1 = (bf16[1,32,64,128]{3,2,1,0:T(8,128)(2,1)S(1)}, bf16[1,32,64,128]{3,2,1,0:T(8,128)(2,1)}, u32[]{:S(2)}) copy-start(bf16[1,32,64,128]{3,2,1,0:T(8,128)(2,1)} %param.5) | copy-start | bytes 1572868
  20.0 5.8 %collective-permute-start.3 = (bf16[34,1,128]{2,1,0:T(2,128)(2,1)S(1)}, bf16[34,1,128]{2,1,0:T(2,128)(2,1)S(1)}, u32[]{:S(2)}, u32[]{:S(2)}) collective-permute-start(bf16[34,1,128]{2,1,0:T(2,128)(2,1)S(1)} %get-tuple-element.19), channel_id=1, source_target_pairs={{1,0},{2,1},{3,2},{5,4},{6,5},{7,6},{9,8},{10,9},{11,10},{13,12},{... | collective-permute-start | bytes 26120 | tf_op jit(solution)/shard_map/ppermute | solution.py:15
  29.2 5.4 %copy-start.7 = (bf16[1,16,32,256]{3,2,1,0:T(8,128)(2,1)S(1)}, bf16[1,16,32,256]{3,2,1,0:T(8,128)(2,1)}, u32[]{:S(2)}) copy-start(bf16[1,16,32,256]{3,2,1,0:T(8,128)(2,1)} %param.9) | copy-start | bytes 786436
  29.3 13.0 %copy-start.2 = (bf16[3,3,256,256]{3,2,1,0:T(8,128)(2,1)S(1)}, bf16[3,3,256,256]{3,2,1,0:T(8,128)(2,1)}, u32[]{:S(2)}) copy-start(bf16[3,3,256,256]{3,2,1,0:T(8,128)(2,1)} %param.8) | copy-start | bytes 3538948
  30.4 5.9 %collective-permute-start.4 = (bf16[1,32,256]{2,1,0:T(8,128)(2,1)S(1)}, bf16[1,32,256]{2,1,0:T(8,128)(2,1)S(1)}, u32[]{:S(2)}, u32[]{:S(2)}) collective-permute-start(bf16[1,32,256]{2,1,0:T(8,128)(2,1)S(1)} %get-tuple-element.52), channel_id=1, source_target_pairs={{0,4},{4,8},{8,12},{1,5},{5,9},{9,13},{2,6},{6,10},{10,14},{3,7},{... | collective-permute-start | bytes 49160 | tf_op jit(solution)/shard_map/ppermute | solution.py:14
  33.4 4.0 %collective-permute-start.5 = (bf16[1,32,256]{2,1,0:T(8,128)(2,1)S(1)}, bf16[1,32,256]{2,1,0:T(8,128)(2,1)S(1)}, u32[]{:S(2)}, u32[]{:S(2)}) collective-permute-start(bf16[1,32,256]{2,1,0:T(8,128)(2,1)S(1)} %get-tuple-element.53), channel_id=1, source_target_pairs={{4,0},{8,4},{12,8},{5,1},{9,5},{13,9},{6,2},{10,6},{14,10},{7,3},{... | collective-permute-start | bytes 49160 | tf_op jit(solution)/shard_map/ppermute | solution.py:15
  34.7 14.0 %collective-permute-start.9 = (bf16[16,32,256]{2,1,0:T(8,128)(2,1)S(1)}, bf16[16,32,256]{2,1,0:T(8,128)(2,1)S(1)}, u32[]{:S(2)}, u32[]{:S(2)}) collective-permute-start(bf16[16,32,256]{2,1,0:T(8,128)(2,1)S(1)} %bitcast.331), channel_id=1, source_target_pairs={{0,16},{16,0},{1,17},{17,1},{2,18},{18,2},{3,19},{19,3},{4,20},{20... | collective-permute-start | bytes 786440 | tf_op jit(solution)/shard_map/ppermute | solution.py:27
  37.5 5.1 %collective-permute-start.6 = (bf16[18,1,256]{2,1,0:T(2,128)(2,1)S(1)}, bf16[18,1,256]{2,1,0:T(2,128)(2,1)S(1)}, u32[]{:S(2)}, u32[]{:S(2)}) collective-permute-start(bf16[18,1,256]{2,1,0:T(2,128)(2,1)S(1)} %get-tuple-element.44), channel_id=1, source_target_pairs={{0,1},{1,2},{2,3},{4,5},{5,6},{6,7},{8,9},{9,10},{10,11},{12,13},{... | collective-permute-start | bytes 27656 | tf_op jit(solution)/shard_map/ppermute | solution.py:14
  40.9 5.7 %collective-permute-start.7 = (bf16[18,1,256]{2,1,0:T(2,128)(2,1)S(1)}, bf16[18,1,256]{2,1,0:T(2,128)(2,1)S(1)}, u32[]{:S(2)}, u32[]{:S(2)}) collective-permute-start(bf16[18,1,256]{2,1,0:T(2,128)(2,1)S(1)} %get-tuple-element.45), channel_id=1, source_target_pairs={{1,0},{2,1},{3,2},{5,4},{6,5},{7,6},{9,8},{10,9},{11,10},{13,12},{... | collective-permute-start | bytes 27656 | tf_op jit(solution)/shard_map/ppermute | solution.py:15
  49.4 6.8 %collective-permute-start.10 = (bf16[1,32,256]{2,1,0:T(8,128)(2,1)S(1)}, bf16[1,32,256]{2,1,0:T(8,128)(2,1)S(1)}, u32[]{:S(2)}, u32[]{:S(2)}) collective-permute-start(bf16[1,32,256]{2,1,0:T(8,128)(2,1)S(1)} %get-tuple-element.48), channel_id=1, source_target_pairs={{0,4},{4,8},{8,12},{1,5},{5,9},{9,13},{2,6},{6,10},{10,14},{3,7},{... | collective-permute-start | bytes 49160 | tf_op jit(solution)/shard_map/ppermute | solution.py:14
  52.6 3.9 %collective-permute-start.11 = (bf16[1,32,256]{2,1,0:T(8,128)(2,1)S(1)}, bf16[1,32,256]{2,1,0:T(8,128)(2,1)S(1)}, u32[]{:S(2)}, u32[]{:S(2)}) collective-permute-start(bf16[1,32,256]{2,1,0:T(8,128)(2,1)S(1)} %get-tuple-element.49), channel_id=1, source_target_pairs={{4,0},{8,4},{12,8},{5,1},{9,5},{13,9},{6,2},{10,6},{14,10},{7,3},{... | collective-permute-start | bytes 49160 | tf_op jit(solution)/shard_map/ppermute | solution.py:15
  56.1 7.9 %copy-start.3 = (f32[9,256,256]{2,1,0:T(8,128)}, f32[9,256,256]{2,1,0:T(8,128)S(1)}, u32[]{:S(2)}) copy-start(f32[9,256,256]{2,1,0:T(8,128)S(1)} %fusion.4) | copy-start | bytes 7077892
  56.5 6.3 %collective-permute-start.12 = (bf16[18,1,256]{2,1,0:T(2,128)(2,1)S(1)}, bf16[18,1,256]{2,1,0:T(2,128)(2,1)S(1)}, u32[]{:S(2)}, u32[]{:S(2)}) collective-permute-start(bf16[18,1,256]{2,1,0:T(2,128)(2,1)S(1)} %get-tuple-element.40), channel_id=1, source_target_pairs={{1,0},{2,1},{3,2},{5,4},{6,5},{7,6},{9,8},{10,9},{11,10},{13,12},{... | collective-permute-start | bytes 27656 | tf_op jit(solution)/shard_map/ppermute | solution.py:15
  57.8 6.0 %collective-permute-start.13 = (bf16[18,1,256]{2,1,0:T(2,128)(2,1)S(1)}, bf16[18,1,256]{2,1,0:T(2,128)(2,1)S(1)}, u32[]{:S(2)}, u32[]{:S(2)}) collective-permute-start(bf16[18,1,256]{2,1,0:T(2,128)(2,1)S(1)} %get-tuple-element.41), channel_id=1, source_target_pairs={{0,1},{1,2},{2,3},{4,5},{5,6},{6,7},{8,9},{9,10},{10,11},{12,13},{... | collective-permute-start | bytes 27656 | tf_op jit(solution)/shard_map/ppermute | solution.py:14
  71.6 0.8 copy-start.4
  72.5 193.3 %all-reduce.7.cloned.1.call-start = ((), (), s32[]{:S(2)}) async-start(), calls=%async_computation.1 | async-start | bytes 6160384 | tf_op jit(solution)/shard_map/psum | solution.py:139
  179.5 6.7 %collective-permute-start.8 = (bf16[16,32,256]{2,1,0:T(8,128)(2,1)S(1)}, bf16[16,32,256]{2,1,0:T(8,128)(2,1)S(1)}, u32[]{:S(2)}, u32[]{:S(2)}) collective-permute-start(bf16[16,32,256]{2,1,0:T(8,128)(2,1)S(1)} %bitcast.332), channel_id=1, source_target_pairs={{0,16},{16,0},{1,17},{17,1},{2,18},{18,2},{3,19},{19,3},{4,20},{20... | collective-permute-start | bytes 786440 | tf_op jit(solution)/shard_map/ppermute | solution.py:27
  265.8 2.6 copy-start.6
Sparse Core Ops, SparseCore 0:
  72.6 106.8 all-reduce.4
  182.0 83.7 all-reduce.6
